TPU v7x, 32 devices: a whole 2x2x4 slice. The times are simulated.
32 devices in a mesh: dp: 4 (over x, core), expert: 2 (over y), etp: 4 (over z).
Axes of the slice: x: 2, y: 2, z: 4, core: 2. Of those that a mesh axis runs over, the one named last changes fastest.
Arguments:
- tokens: bfloat16 [1024, 6144], P(('dp', 'expert'), 'etp'), may hold values from -6 to 6
- routes: int32 [1024, 2], P(('dp', 'expert')), may hold values from 0 to 1, as said below
- gate_scale: float32 [1024, 2], P(('dp', 'expert')), may hold values from 0.2 to 1
- gate_weight: bfloat16 [2, 128, 6, 128, 128], P('expert', 'etp'), may hold values from -0.21875 to 0.21875
- up_weight: bfloat16 [2, 128, 6, 128, 128], P('expert', 'etp'), may hold values from -0.21875 to 0.21875
- down_weight: bfloat16 [2, 16, 48, 128, 128], P('expert', 'etp'), may hold values from -0.125 to 0.125
- gate_blocks: int32 [2, 128, 6], P('expert', 'etp'), may hold values from 0 to 47, as said below
- down_blocks: int32 [2, 16, 48], P('expert', 'etp'), may hold values from 0 to 7
Outputs:
- mixed: bfloat16 [1024, 6144], P(('dp', 'expert'), 'etp')
Inputs may be any that keep to these rules, and one draw needn't show every extreme that they name: `routes`: the two entries of a token name different experts. In each aligned block of 128 rows no expert is named more than 128 times, and one expert, the same for all blocks, is named exactly 128 times in every block. `gate_blocks`: for each expert and hidden block the 6 entries are different.
All inputs are finite; a program needn't handle non-finite values.
Results may differ from a plain program's by a relative error of at most 0.011.
Values may be sent and summed in bfloat16 or wider, within the bound.
No kernel may reach another device: no remote copies, remote signals or barrier semaphores. Data moves between devices by JAX's collectives and lax.ppermute only.
A program may use at most 128 MiB of HBM per device.

v0:
```python
import jax
import jax.numpy as jnp
from jax import lax
from jax.sharding import PartitionSpec as P


def slot_places(route_rows, expert_count, capacity):
    flat_routes = route_rows.reshape(-1)
    onehot = (flat_routes[:, None] == jnp.arange(expert_count, dtype=jnp.int32)[None, :]).astype(
        jnp.int32
    )
    earlier = jnp.cumsum(onehot, axis=0) - onehot
    slot_place = jnp.sum(earlier * onehot, axis=1)
    return flat_routes * capacity + slot_place


def expert_layer(token_rows, gate_part, up_part, down_part, gate_pick, down_pick):
    row_count = token_rows.shape[0]
    model_width = token_rows.shape[1]
    block_size = gate_part.shape[-1]
    hidden_count = gate_part.shape[0]
    keep_count = gate_part.shape[1]
    group_count = down_part.shape[0]
    group_size = hidden_count // group_count
    tiles = token_rows.reshape(row_count, model_width // block_size, block_size)
    picked = jnp.take(tiles, gate_pick.reshape(-1), axis=1).reshape(
        row_count, hidden_count, keep_count, block_size
    )
    gate_act = jnp.einsum("rfki,fkio->rfo", picked, gate_part, preferred_element_type=jnp.float32)
    up_act = jnp.einsum("rfki,fkio->rfo", picked, up_part, preferred_element_type=jnp.float32)
    hidden = (jax.nn.silu(gate_act) * up_act).astype(jnp.bfloat16)
    sources = down_pick + (jnp.arange(group_count, dtype=jnp.int32) * group_size)[:, None]
    chosen = jnp.take(hidden, sources.reshape(-1), axis=1).reshape(
        row_count, group_count, model_width // block_size, block_size
    )
    partial_value = jnp.einsum(
        "rgbi,gbio->rbo", chosen, down_part, preferred_element_type=jnp.float32
    )
    return partial_value.reshape(row_count, model_width)


def body(tokens, routes, gate_scale, gate_weight, up_weight, down_weight, gate_blocks, down_blocks):
    tok_count = tokens.shape[0]
    local_width = tokens.shape[1]
    group_total = lax.axis_size("expert")
    capacity = min(tok_count, 5 * tok_count // (2 * group_total))
    destination = slot_places(routes, group_total, capacity)
    filler = jnp.full((group_total * capacity,), tok_count, jnp.int32)
    anchor = filler.at[destination].set(jnp.arange(2 * tok_count, dtype=jnp.int32) // 2)
    outgoing = jnp.take(tokens, anchor, axis=0, mode="fill", fill_value=0)
    outgoing = outgoing.reshape(group_total, capacity, local_width)
    incoming = lax.all_to_all(outgoing, "expert", split_axis=0, concat_axis=0, tiled=True)
    arrived = lax.all_gather(incoming, "etp", axis=2, tiled=True)
    full_width = arrived.shape[2]
    partial_value = expert_layer(
        arrived.reshape(group_total * capacity, full_width),
        gate_weight[0],
        up_weight[0],
        down_weight[0],
        gate_blocks[0],
        down_blocks[0],
    )
    partial_value = partial_value.reshape(group_total, capacity, full_width)
    summed = lax.psum_scatter(
        partial_value.astype(jnp.bfloat16), "etp", scatter_dimension=2, tiled=True
    )
    returned = lax.all_to_all(summed, "expert", split_axis=0, concat_axis=0, tiled=True)
    returned = returned.reshape(group_total * capacity, local_width)
    fetched = (
        jnp.take(returned, destination, axis=0)
        .reshape(tok_count, 2, local_width)
        .astype(jnp.float32)
    )
    mixed = jnp.sum(fetched * gate_scale[:, :, None], axis=1)
    return mixed.astype(jnp.bfloat16)


def solution(mesh):
    placed = (
        P(("dp", "expert"), "etp"),
        P(("dp", "expert"), None),
        P(("dp", "expert"), None),
        P("expert", "etp", None, None, None),
        P("expert", "etp", None, None, None),
        P("expert", "etp", None, None, None),
        P("expert", "etp", None),
        P("expert", "etp", None),
    )
    return jax.shard_map(
        body, mesh=mesh, in_specs=placed, out_specs=P(("dp", "expert"), "etp"), check_vma=False
    )
```

profile of v0, /device:TPU:0, one launch (start us, length us, event | category | flops | bytes accessed | tf_op | source)
XLA Modules:
  0.0 239.1 jit_solution(16709429015321153645)
XLA Ops:
  6.5 0.8 copy.36
  7.4 0.1 eq.26
  7.5 0.1 reshape.162
  7.7 0.7 broadcast_multiply_fusion
  8.4 0.6 reduce-window.6
  9.0 0.2 slice_reduce_fusion
  9.2 0.2 reduce-window.9
  9.4 0.1 add_bitcast_fusion
  9.4 0.1 copy.42
  9.6 0.1 mul.46
  9.7 1.4 scatter_custom_fusion
  11.2 1.3 gather_fusion
  12.5 0.1 broadcast_select_fusion.6
  12.6 15.5 %all_to_all.10 = bf16[2,128,1536]{2,1,0:T(8,128)(2,1)} all-to-all(bf16[2,128,1536]{2,1,0:T(8,128)(2,1)S(1)} %broadcast_select_fusion.6), channel_id=1, replica_groups=mesh['dp'=4,'expert'=2,'etp'=4] {'expert'}, dimensions={0} | all-to-all | bytes 1572864 | tf_op jit(solution)/shard_map/all_to_all | solution.py:52
  28.1 0.0 all-gather.2.cloned.1.call-update
  28.1 0.2 reduce-scatter.2.cloned.1.call-start
  28.3 0.1 copy.43
  28.4 0.1 reshape_squeeze.6
  28.6 0.1 copy.41
  28.7 0.1 add.124
  28.7 0.1 add.137
  28.8 0.1 squeeze.17
  28.9 0.1 compare_and_fusion.1
  29.0 0.1 copy.40
  29.1 63.1 %all-gather.2.cloned.1.call-done = bf16[2,128,6144]{2,1,0:T(8,128)(2,1)} async-done(((bf16[2,128,1536]{2,1,0:T(8,128)(2,1)}), bf16[2,128,6144]{2,1,0:T(8,128)(2,1)}) %all-gather.2.cloned.1.call-update) | async-done | bytes 3145744 | tf_op jit(solution)/shard_map/all_gather | solution.py:53
  92.2 2.6 %copy.54 = bf16[32,8,48,128]{3,2,1,0:T(8,128)(2,1)S(1)} copy(bf16[32,8,48,128]{3,1,2,0:T(8,128)(2,1)} %bitcast.93) | data formatting | bytes 6291456
  94.8 0.8 copy.44
  95.7 8.2 %gather_fusion.1 = bf16[192,256,128]{2,1,0:T(8,128)(2,1)} fusion(bf16[256,48,128]{2,0,1:T(8,128)(2,1)S(1)} %copy.44, s32[1024]{0:T(1024)S(1)} %pad_clamp_fusion.2), kind=kCustom, calls=%fused_computation.1 | custom fusion | bytes 25166592 | tf_op jit(solution)/shard_map/jit(_take)/gather | solution.py:26
  103.9 11.8 %fusion.3 = f32[32,256,128,1]{2,1,3,0:T(8,128)} fusion(bf16[256,32,6,128]{3,0,2,1:T(8,128)(2,1)} %bitcast.89, pred[32,6]{1,0:T(8,128)(4,1)S(1)} %copy.41, bf16[1,32,6,128,128]{4,3,2,1,0:T(8,128)(2,1)} %param.11), kind=kOutput, calls=%fused_computation.10 | convolution fusion | flops 1616904192 | bytes 23068864 | tf_op jit(solution)/shard_map/rfki,fkio->rfo/dot_general | solution.py:29
  115.7 11.1 %fusion.10 = bf16[256,32,128]{2,0,1:T(8,128)(2,1)S(1)} fusion(f32[32,256,128,1]{2,1,3,0:T(8,128)} %fusion.3, bf16[1,32,6,128,128]{4,3,2,1,0:T(8,128)(2,1)} %param.12, bf16[256,32,6,128]{3,0,2,1:T(8,128)(2,1)} %bitcast.90, pred[32,6]{1,0:T(8,128)(4,1)S(1)} %copy.41), kind=kOutput, calls=%fused_computation.19 | convolution fusion | flops 1623195648 | bytes 25166016 | tf_op jit(solution)/shard_map/rfki,fkio->rfo/dot_general | solution.py:30
  126.8 8.2 %gather_fusion.2 = bf16[192,256,128]{2,1,0:T(8,128)(2,1)} fusion(bf16[256,32,128]{2,0,1:T(8,128)(2,1)S(1)} %fusion.10, s32[1024]{0:T(1024)S(1)} %pad_clamp_fusion.1), kind=kCustom, calls=%fused_computation.2 | custom fusion | bytes 25166592 | tf_op jit(solution)/shard_map/jit(_take)/gather | solution.py:33
  135.1 11.5 %fusion.14 = bf16[256,48,128]{2,0,1:T(8,128)(2,1)} fusion(bf16[256,4,48,128]{3,0,2,1:T(8,128)(2,1)} %bitcast.91, pred[4,48]{0,1:T(8,128)(4,1)S(1)} %copy.40, bf16[1,4,48,128,128]{4,3,2,1,0:T(8,128)(2,1)} %param.13), kind=kOutput, calls=%fused_computation.25 | convolution fusion | flops 1618477056 | bytes 22020288 | tf_op jit(solution)/shard_map/rgbi,gbio->rbo/dot_general | solution.py:36
  146.6 3.9 %copy.47 = bf16[256,48,128]{2,1,0:T(8,128)(2,1)S(1)} copy(bf16[256,48,128]{2,0,1:T(8,128)(2,1)} %fusion.14) | data formatting | bytes 6291456 | tf_op jit(solution)/shard_map/convert_element_type | solution.py:65
  150.5 0.0 copy-start.3
  150.5 0.0 copy-start.5
  150.5 2.8 %convert_element_type.30 = bf16[2,128,6144]{2,1,0:T(8,128)(2,1)} reshape(bf16[256,48,128]{2,1,0:T(8,128)(2,1)S(1)} %copy.47) | data formatting | bytes 6291456 | tf_op jit(solution)/shard_map/convert_element_type | solution.py:65
  153.4 0.0 reduce-scatter.2.cloned.1.call-update
  153.4 0.0 copy-start.1
  153.4 59.2 %reduce-scatter.2.cloned.1.call-done = bf16[2,128,1536]{2,1,0:T(8,128)(2,1)} async-done(((bf16[2,128,6144]{2,1,0:T(8,128)(2,1)}), bf16[2,128,1536]{2,1,0:T(8,128)(2,1)}) %reduce-scatter.2.cloned.1.call-update) | async-done | bytes 786448 | tf_op jit(solution)/shard_map/reduce_scatter | solution.py:64
  212.6 3.5 %all-to-all-start.1 = ((bf16[2,128,1536]{2,1,0:T(8,128)(2,1)}), bf16[2,128,1536]{2,1,0:T(8,128)(2,1)S(1)}, u32[]{:S(2)}, u32[]{:S(2)}) async-start(bf16[2,128,1536]{2,1,0:T(8,128)(2,1)} %reduce-scatter.2.cloned.1.call-done), calls=%async_computation.2 | async-start | bytes 1572864 | tf_op jit(solution)/shard_map/all_to_all | solution.py:67
  216.1 0.1 reduce_sum.23
  216.3 0.1 copy.38
  216.4 0.1 copy.39
  216.5 0.1 copy.48
  216.6 10.2 %all-to-all-done.1 = bf16[2,128,1536]{2,1,0:T(8,128)(2,1)S(1)} async-done(((bf16[2,128,1536]{2,1,0:T(8,128)(2,1)}), bf16[2,128,1536]{2,1,0:T(8,128)(2,1)S(1)}, u32[]{:S(2)}, u32[]{:S(2)}) %all-to-all-start.1) | async-done | bytes 786464 | tf_op jit(solution)/shard_map/all_to_all | solution.py:67
  226.8 1.3 gather_fusion.3
  228.0 0.3 gather.31
  228.4 3.9 %multiply_reduce_fusion = bf16[128,1536]{1,0:T(8,128)(2,1)} fusion(bf16[128,2,1536]{2,1,0:T(2,128)(2,1)S(1)} %gather.31, pred[128,2]{1,0:T(8,128)(4,1)S(1)} %copy.39, f32[128,2]{1,0:T(8,128)S(1)} %copy.48), kind=kLoop, calls=%fused_computation.26 | loop fusion | flops 1376256 | bytes 1180928 | tf_op jit(solution)/shard_map/reduce_sum | solution.py:74
  (25 shorter events, 0.1 us)
Async XLA Ops:
  6.5 4.7 %copy-start = (bf16[128,1536]{1,0:T(8,128)(2,1)S(1)}, bf16[128,1536]{1,0:T(8,128)(2,1)}, u32[]{:S(2)}) copy-start(bf16[128,1536]{1,0:T(8,128)(2,1)} %param.8) | copy-start | bytes 1179652
  6.5 21.8 %copy-start.2 = (s32[1,32,6]{1,0,2:T(1,128)S(1)}, s32[1,32,6]{1,0,2:T(1,128)}, u32[]{:S(2)}) copy-start(s32[1,32,6]{1,0,2:T(1,128)} %param.14) | copy-start | bytes 2308
  6.5 22.3 %copy-start.4 = (s32[1,4,48]{2,1,0:T(4,128)S(1)}, s32[1,4,48]{2,1,0:T(4,128)}, u32[]{:S(2)}) copy-start(s32[1,4,48]{2,1,0:T(4,128)} %param.15) | copy-start | bytes 2308
  6.5 85.7 %all-gather.2.cloned.1.call-start = ((), (), s32[]{:S(2)}) async-start(), calls=%async_computation.3 | async-start | bytes 3932160 | tf_op jit(solution)/shard_map/all_gather | solution.py:53
  28.1 184.5 %reduce-scatter.2.cloned.1.call-start = ((), (), s32[]{:S(2)}) async-start(), calls=%async_computation.4 | async-start | bytes 3932160 | tf_op jit(solution)/shard_map/reduce_scatter | solution.py:64
  150.5 65.8 %copy-start.3 = (s32[128,2]{0,1:T(2,128)S(1)}, s32[128,2]{0,1:T(2,128)}, u32[]{:S(2)}) copy-start(s32[128,2]{0,1:T(2,128)} %param.9) | copy-start | bytes 3076
  150.5 66.0 %copy-start.5 = (f32[128,2]{0,1:T(2,128)S(1)}, f32[128,2]{0,1:T(2,128)}, u32[]{:S(2)}) copy-start(f32[128,2]{0,1:T(2,128)} %param.10) | copy-start | bytes 3076
  153.4 78.8 %copy-start.1 = (bf16[128,1536]{1,0:T(8,128)(2,1)S(1)}, bf16[128,1536]{1,0:T(8,128)(2,1)}, u32[]{:S(2)}) copy-start(bf16[128,1536]{1,0:T(8,128)(2,1)} %param.8) | copy-start | bytes 1179652
  212.6 14.2 %all-to-all-start.1 = ((bf16[2,128,1536]{2,1,0:T(8,128)(2,1)}), bf16[2,128,1536]{2,1,0:T(8,128)(2,1)S(1)}, u32[]{:S(2)}, u32[]{:S(2)}) async-start(bf16[2,128,1536]{2,1,0:T(8,128)(2,1)} %reduce-scatter.2.cloned.1.call-done), calls=%async_computation.2 | async-start | bytes 1572864 | tf_op jit(solution)/shard_map/all_to_all | solution.py:67
Sparse Core Ops, SparseCore 0:
  28.2 63.9 all-gather.1
  153.5 59.0 reduce-scatter.1
where the time goes:
time: 239 us
  waiting for transfers between devices  132 us (55%)
  matrix products  34.5 us (14%)
  local copies, waits for them, and re-layouts  33.6 us (14%)
  blocking collectives  15.5 us (6%)
  between operations  13.6 us (6%)
  other arithmetic  5.75 us (2%)
  starting transfers between devices  3.76 us (2%)
    all_gather x1, waiting for transfers between devices, body(): arrived = lax.all_gather(incoming, 'etp', axis=2, tiled=True)  63.1 us
    reduce_scatter x1, waiting for transfers between devices, body(): lax.psum_scatter(partial_value.astype(jnp.bfloat16), 'etp', scatter_dimen...  59.2 us
    all_to_all x1, blocking collectives, body(): lax.all_to_all(outgoing, 'expert', split_axis=0, concat_axis=0, tiled=True)  15.5 us
    dot_general x1, matrix products, expert_layer(): jnp.einsum('rfki,fkio->rfo', picked, gate_part, preferred_element_type=jn...  11.8 us
    dot_general x1, matrix products, expert_layer(): jnp.einsum('rgbi,gbio->rbo', chosen, down_part, preferred_element_type=jn...  11.5 us
    dot_general x1, matrix products, expert_layer(): jnp.einsum('rfki,fkio->rfo', picked, up_part, preferred_element_type=jnp....  11.1 us
    all_to_all x1, waiting for transfers between devices, body(): lax.all_to_all(summed, 'expert', split_axis=0, concat_axis=0, tiled=True)  10.2 us
    gather x1, local copies, waits for them, and re-layouts, expert_layer(): jnp.take(hidden, sources.reshape(-1), axis=1)  8.24 us
  transfers between devices with their start and end apart: 3, of which 3 were waited for; matrix products, arithmetic and copies ran while one was open for 1% of the time, Pallas kernels for 0%

commit v1 on v0

--- a/solution.py
+++ b/solution.py
@@ -50,7 +50,12 @@
     outgoing = jnp.take(tokens, anchor, axis=0, mode="fill", fill_value=0)
     outgoing = outgoing.reshape(group_total, capacity, local_width)
     incoming = lax.all_to_all(outgoing, "expert", split_axis=0, concat_axis=0, tiled=True)
-    arrived = lax.all_gather(incoming, "etp", axis=2, tiled=True)
+    ring = [incoming]
+    for hop in range(3):
+        ring.append(lax.ppermute(ring[-1], "etp", [(dev, (dev + 1) % 4) for dev in range(4)]))
+    arrived = jnp.roll(
+        jnp.concatenate(ring[::-1], axis=2), (lax.axis_index("etp") + 1) * ring[0].shape[2], axis=2
+    )
     full_width = arrived.shape[2]
     partial_value = expert_layer(
         arrived.reshape(group_total * capacity, full_width),

time: 239 us -> 232 us (0.971)
  waiting for transfers between devices: 132 us -> 124 us
    all_gather x1 -> x0, waiting for transfers between devices: 63.1 us -> none  [body(): arrived = lax.all_gather(incoming, 'etp', axis=2, tiled=True)]
    ppermute x0 -> x3, waiting for transfers between devices: none -> 55.7 us  [body(): lax.ppermute(ring[-1], 'etp', [(dev, (dev + 1) % 4) for dev in range(4)])]
  transfers between devices with their start and end apart: 3 -> 5, of which waited for: 3 -> 5; matrix products, arithmetic and copies ran while one was open for 1% -> 1% of each run, Pallas kernels for 0% -> 0%
where the time goes in v1:
time: 232 us
  waiting for transfers between devices  124 us (53%)
  matrix products  34.4 us (15%)
  local copies, waits for them, and re-layouts  33.8 us (15%)
  blocking collectives  14.8 us (6%)
  between operations  13.7 us (6%)
  other arithmetic  5.75 us (2%)
  starting transfers between devices  5.25 us (2%)
    reduce_scatter x1, waiting for transfers between devices, body(): lax.psum_scatter(partial_value.astype(jnp.bfloat16), 'etp', scatter_dimen...  58.2 us
    ppermute x3, waiting for transfers between devices, body(): lax.ppermute(ring[-1], 'etp', [(dev, (dev + 1) % 4) for dev in range(4)])  55.7 us
    all_to_all x1, blocking collectives, body(): lax.all_to_all(outgoing, 'expert', split_axis=0, concat_axis=0, tiled=True)  14.8 us
    dot_general x1, matrix products, expert_layer(): jnp.einsum('rfki,fkio->rfo', picked, gate_part, preferred_element_type=jn...  11.8 us
    dot_general x1, matrix products, expert_layer(): jnp.einsum('rgbi,gbio->rbo', chosen, down_part, preferred_element_type=jn...  11.5 us
    dot_general x1, matrix products, expert_layer(): jnp.einsum('rfki,fkio->rfo', picked, up_part, preferred_element_type=jnp....  11.1 us
    all_to_all x1, waiting for transfers between devices, body(): lax.all_to_all(summed, 'expert', split_axis=0, concat_axis=0, tiled=True)  10.1 us
    gather x1, local copies, waits for them, and re-layouts, expert_layer(): jnp.take(tiles, gate_pick.reshape(-1), axis=1)  8.42 us
  transfers between devices with their start and end apart: 5, of which 5 were waited for; matrix products, arithmetic and copies ran while one was open for 1% of the time, Pallas kernels for 0%

profile of v1, /device:TPU:0, one launch (start us, length us, event | category | flops | bytes accessed | tf_op | source)
XLA Modules:
  0.0 231.8 jit_solution(1701957925171940458)
XLA Ops:
  6.5 0.8 copy.36
  7.4 0.1 eq.29
  7.5 0.1 reshape.162
  7.7 0.7 broadcast_multiply_fusion
  8.4 0.6 reduce-window.6
  9.0 0.2 slice_reduce_fusion
  9.2 0.2 reduce-window.9
  9.4 0.1 copy.42
  9.6 0.1 mul.49
  9.7 1.4 scatter_custom_fusion
  11.2 1.3 gather_fusion
  12.5 0.1 broadcast_select_fusion.6
  12.6 14.8 %all_to_all.10 = bf16[2,128,1536]{2,1,0:T(8,128)(2,1)S(1)} all-to-all(bf16[2,128,1536]{2,1,0:T(8,128)(2,1)S(1)} %broadcast_select_fusion.6), channel_id=1, replica_groups=mesh['dp'=4,'expert'=2,'etp'=4] {'expert'}, dimensions={0} | all-to-all | bytes 1572864 | tf_op jit(solution)/shard_map/all_to_all | solution.py:52
  27.4 1.7 collective-permute-start
  29.1 18.6 %collective-permute-done = bf16[2,128,1536]{2,1,0:T(8,128)(2,1)S(1)} collective-permute-done((bf16[2,128,1536]{2,1,0:T(8,128)(2,1)S(1)}, bf16[2,128,1536]{2,1,0:T(8,128)(2,1)S(1)}, u32[]{:S(2)}, u32[]{:S(2)}) %collective-permute-start) | collective-permute-done | bytes 786464 | tf_op jit(solution)/shard_map/ppermute | solution.py:55
  47.7 19.4 %collective-permute-done.1 = bf16[2,128,1536]{2,1,0:T(8,128)(2,1)S(1)} collective-permute-done((bf16[2,128,1536]{2,1,0:T(8,128)(2,1)S(1)}, bf16[2,128,1536]{2,1,0:T(8,128)(2,1)S(1)}, u32[]{:S(2)}, u32[]{:S(2)}) %collective-permute-start.1) | collective-permute-done | bytes 786464 | tf_op jit(solution)/shard_map/ppermute | solution.py:55
  67.1 0.1 copy.43
  67.4 0.1 reshape_squeeze.6
  67.5 0.1 copy.41
  67.7 0.1 copy.40
  67.9 17.8 %collective-permute-done.2 = bf16[2,128,1536]{2,1,0:T(8,128)(2,1)S(1)} collective-permute-done((bf16[2,128,1536]{2,1,0:T(8,128)(2,1)S(1)}, bf16[2,128,1536]{2,1,0:T(8,128)(2,1)S(1)}, u32[]{:S(2)}, u32[]{:S(2)}) %collective-permute-start.2) | collective-permute-done | bytes 786464 | tf_op jit(solution)/shard_map/ppermute | solution.py:55
  85.6 0.1 constant_dynamic-update-slice_fusion.7
  85.7 0.1 constant_dynamic-update-slice_fusion.6
  85.9 0.1 constant_dynamic-update-slice_fusion.5
  86.0 0.1 constant_dynamic-update-slice_fusion.4
  86.1 0.1 constant_dynamic-update-slice_fusion.3
  86.2 0.1 constant_dynamic-update-slice_fusion.2
  86.3 0.1 constant_dynamic-update-slice_fusion.1
  86.4 0.1 constant_dynamic-update-slice_fusion
  86.5 1.2 constant_dynamic-slice_fusion
  87.7 0.7 copy.54
  88.4 0.8 copy.44
  89.2 8.4 %gather_fusion.1 = bf16[192,256,128]{2,1,0:T(8,128)(2,1)} fusion(bf16[256,48,128]{2,0,1:T(8,128)(2,1)S(1)} %copy.44, s32[1024]{0:T(1024)S(1)} %get-tuple-element.6), kind=kCustom, calls=%fused_computation.1 | custom fusion | bytes 25166592 | tf_op jit(solution)/shard_map/jit(_take)/gather | solution.py:26
  97.7 11.8 %fusion.3 = f32[32,256,128,1]{2,1,3,0:T(8,128)} fusion(bf16[256,32,6,128]{3,0,2,1:T(8,128)(2,1)} %bitcast.89, pred[32,6]{1,0:T(8,128)(4,1)S(1)} %copy.41, bf16[1,32,6,128,128]{4,3,2,1,0:T(8,128)(2,1)} %param.11), kind=kOutput, calls=%fused_computation.10 | convolution fusion | flops 1616904192 | bytes 23068864 | tf_op jit(solution)/shard_map/rfki,fkio->rfo/dot_general | solution.py:29
  109.5 11.1 %fusion.10 = bf16[256,32,128]{2,0,1:T(8,128)(2,1)S(1)} fusion(f32[32,256,128,1]{2,1,3,0:T(8,128)} %fusion.3, bf16[1,32,6,128,128]{4,3,2,1,0:T(8,128)(2,1)} %param.12, bf16[256,32,6,128]{3,0,2,1:T(8,128)(2,1)} %bitcast.90, pred[32,6]{1,0:T(8,128)(4,1)S(1)} %copy.41), kind=kOutput, calls=%fused_computation.19 | convolution fusion | flops 1623195648 | bytes 25166016 | tf_op jit(solution)/shard_map/rfki,fkio->rfo/dot_general | solution.py:30
  120.6 8.2 %gather_fusion.2 = bf16[192,256,128]{2,1,0:T(8,128)(2,1)} fusion(bf16[256,32,128]{2,0,1:T(8,128)(2,1)S(1)} %fusion.10, s32[1024]{0:T(1024)S(1)} %get-tuple-element.5), kind=kCustom, calls=%fused_computation.2 | custom fusion | bytes 25166592 | tf_op jit(solution)/shard_map/jit(_take)/gather | solution.py:33
  128.8 11.5 %fusion.14 = bf16[256,48,128]{2,0,1:T(8,128)(2,1)} fusion(bf16[256,4,48,128]{3,0,2,1:T(8,128)(2,1)} %bitcast.91, pred[4,48]{0,1:T(8,128)(4,1)S(1)} %copy.40, bf16[1,4,48,128,128]{4,3,2,1,0:T(8,128)(2,1)} %param.13), kind=kOutput, calls=%fused_computation.25 | convolution fusion | flops 1618477056 | bytes 22020288 | tf_op jit(solution)/shard_map/rgbi,gbio->rbo/dot_general | solution.py:36
  140.3 3.9 %copy.47 = bf16[256,48,128]{2,1,0:T(8,128)(2,1)S(1)} copy(bf16[256,48,128]{2,0,1:T(8,128)(2,1)} %fusion.14) | data formatting | bytes 6291456 | tf_op jit(solution)/shard_map/convert_element_type | solution.py:70
  144.3 2.8 %convert_element_type.30 = bf16[2,128,6144]{2,1,0:T(8,128)(2,1)} reshape(bf16[256,48,128]{2,1,0:T(8,128)(2,1)S(1)} %copy.47) | data formatting | bytes 6291456 | tf_op jit(solution)/shard_map/convert_element_type | solution.py:70
  147.2 58.2 %reduce-scatter.2.cloned.1.call-done = bf16[2,128,1536]{2,1,0:T(8,128)(2,1)} async-done(((bf16[2,128,6144]{2,1,0:T(8,128)(2,1)}), bf16[2,128,1536]{2,1,0:T(8,128)(2,1)}) %reduce-scatter.2.cloned.1.call-update) | async-done | bytes 786448 | tf_op jit(solution)/shard_map/reduce_scatter | solution.py:69
  205.3 3.5 %all-to-all-start.1 = ((bf16[2,128,1536]{2,1,0:T(8,128)(2,1)}), bf16[2,128,1536]{2,1,0:T(8,128)(2,1)S(1)}, u32[]{:S(2)}, u32[]{:S(2)}) async-start(bf16[2,128,1536]{2,1,0:T(8,128)(2,1)} %reduce-scatter.2.cloned.1.call-done), calls=%async_computation.2 | async-start | bytes 1572864 | tf_op jit(solution)/shard_map/all_to_all | solution.py:72
  208.9 0.1 reduce_sum.23
  209.1 0.1 copy.39
  209.2 0.1 copy.48
  209.4 10.1 %all-to-all-done.1 = bf16[2,128,1536]{2,1,0:T(8,128)(2,1)S(1)} async-done(((bf16[2,128,1536]{2,1,0:T(8,128)(2,1)}), bf16[2,128,1536]{2,1,0:T(8,128)(2,1)S(1)}, u32[]{:S(2)}, u32[]{:S(2)}) %all-to-all-start.1) | async-done | bytes 786464 | tf_op jit(solution)/shard_map/all_to_all | solution.py:72
  219.5 1.3 gather_fusion.3
  220.8 0.3 gather.31
  221.1 3.9 %multiply_reduce_fusion = bf16[128,1536]{1,0:T(8,128)(2,1)} fusion(bf16[128,2,1536]{2,1,0:T(2,128)(2,1)S(1)} %gather.31, pred[128,2]{1,0:T(8,128)(4,1)S(1)} %copy.39, f32[128,2]{1,0:T(8,128)S(1)} %copy.48), kind=kLoop, calls=%fused_computation.26 | loop fusion | flops 1376256 | bytes 1180928 | tf_op jit(solution)/shard_map/reduce_sum | solution.py:79
  (36 shorter events, 0.6 us)
Async XLA Ops:
  6.5 4.7 %copy-start = (bf16[128,1536]{1,0:T(8,128)(2,1)S(1)}, bf16[128,1536]{1,0:T(8,128)(2,1)}, u32[]{:S(2)}) copy-start(bf16[128,1536]{1,0:T(8,128)(2,1)} %param.8) | copy-start | bytes 1179652
  6.5 41.2 %copy-start.2 = (s32[1,32,6]{1,0,2:T(1,128)S(1)}, s32[1,32,6]{1,0,2:T(1,128)}, u32[]{:S(2)}) copy-start(s32[1,32,6]{1,0,2:T(1,128)} %param.14) | copy-start | bytes 2308
  6.5 60.8 %copy-start.4 = (s32[1,4,48]{2,1,0:T(4,128)S(1)}, s32[1,4,48]{2,1,0:T(4,128)}, u32[]{:S(2)}) copy-start(s32[1,4,48]{2,1,0:T(4,128)} %param.15) | copy-start | bytes 2308
  6.5 198.8 %reduce-scatter.2.cloned.1.call-start = ((), (), s32[]{:S(2)}) async-start(), calls=%async_computation.3 | async-start | bytes 3932160 | tf_op jit(solution)/shard_map/reduce_scatter | solution.py:69
  27.4 20.3 %collective-permute-start = (bf16[2,128,1536]{2,1,0:T(8,128)(2,1)S(1)}, bf16[2,128,1536]{2,1,0:T(8,128)(2,1)S(1)}, u32[]{:S(2)}, u32[]{:S(2)}) collective-permute-start(bf16[2,128,1536]{2,1,0:T(8,128)(2,1)S(1)} %all_to_all.10), channel_id=1, source_target_pairs={{0,1},{1,2},{2,3},{3,0},{4,5},{5,6},{6,7},{7,4},{8,9},{9,10},{10,1... | collective-permute-start | bytes 2359304 | tf_op jit(solution)/shard_map/ppermute | solution.py:55
  47.7 19.4 %collective-permute-start.1 = (bf16[2,128,1536]{2,1,0:T(8,128)(2,1)S(1)}, bf16[2,128,1536]{2,1,0:T(8,128)(2,1)S(1)}, u32[]{:S(2)}, u32[]{:S(2)}) collective-permute-start(bf16[2,128,1536]{2,1,0:T(8,128)(2,1)S(1)} %collective-permute-done), channel_id=1, source_target_pairs={{0,1},{1,2},{2,3},{3,0},{4,5},{5,6},{6,7},{7,4},{8,9},{9,10},{10,1... | collective-permute-start | bytes 2359304 | tf_op jit(solution)/shard_map/ppermute | solution.py:55
  67.1 18.5 %collective-permute-start.2 = (bf16[2,128,1536]{2,1,0:T(8,128)(2,1)S(1)}, bf16[2,128,1536]{2,1,0:T(8,128)(2,1)S(1)}, u32[]{:S(2)}, u32[]{:S(2)}) collective-permute-start(bf16[2,128,1536]{2,1,0:T(8,128)(2,1)S(1)} %collective-permute-done.1), channel_id=1, source_target_pairs={{0,1},{1,2},{2,3},{3,0},{4,5},{5,6},{6,7},{7,4},{8,9},{9,10},{10,1... | collective-permute-start | bytes 2359304 | tf_op jit(solution)/shard_map/ppermute | solution.py:55
  144.3 64.8 %copy-start.3 = (s32[128,2]{0,1:T(2,128)S(1)}, s32[128,2]{0,1:T(2,128)}, u32[]{:S(2)}) copy-start(s32[128,2]{0,1:T(2,128)} %param.9) | copy-start | bytes 3076
  144.3 65.0 %copy-start.5 = (f32[128,2]{0,1:T(2,128)S(1)}, f32[128,2]{0,1:T(2,128)}, u32[]{:S(2)}) copy-start(f32[128,2]{0,1:T(2,128)} %param.10) | copy-start | bytes 3076
  147.1 77.8 %copy-start.1 = (bf16[128,1536]{1,0:T(8,128)(2,1)S(1)}, bf16[128,1536]{1,0:T(8,128)(2,1)}, u32[]{:S(2)}) copy-start(bf16[128,1536]{1,0:T(8,128)(2,1)} %param.8) | copy-start | bytes 1179652
  205.3 14.2 %all-to-all-start.1 = ((bf16[2,128,1536]{2,1,0:T(8,128)(2,1)}), bf16[2,128,1536]{2,1,0:T(8,128)(2,1)S(1)}, u32[]{:S(2)}, u32[]{:S(2)}) async-start(bf16[2,128,1536]{2,1,0:T(8,128)(2,1)} %reduce-scatter.2.cloned.1.call-done), calls=%async_computation.2 | async-start | bytes 1572864 | tf_op jit(solution)/shard_map/all_to_all | solution.py:72
Sparse Core Ops, SparseCore 0:
  147.3 58.0 reduce-scatter.1
